TPU v7x, 256 devices: a whole 4x4x8 slice. The times are simulated.
256 devices in a mesh: col: 16 (over z, core), row: 16 (over x, y).
Axes of the slice: x: 4, y: 4, z: 8, core: 2. Of those that a mesh axis runs over, the one named last changes fastest.
Arguments:
- lower_cols: float32 [4096, 2048], P('col', 'row'), may hold values from -6 to 6
- pivot_rows: float32 [8192, 4096], P('row', 'col')
- pattern: int32 [64, 32], replicated, may hold values 0 or 1
- panel_in: float32 [8192, 2048], P('col', 'row'), may hold values from -6 to 6
- diag_in: float32 [64, 128, 128], P('col'), as said below
Outputs:
- panel: float32 [8192, 2048], P('col', 'row')
- factor: float32 [64, 128, 128], P('col')
Inputs may be any that keep to these rules, and one draw needn't show every extreme that they name: diag_in holds symmetric blocks with diagonal entries between 2.5 and 4.5; diag_in[j] - dsum[j] is positive definite.
All inputs are finite; a program needn't handle non-finite values.
Results may differ from a plain program's by a relative error of at most 0.00005.
Values sent between devices are 32-bit elements; how exact they have to be, the bound alone decides.
A program may use at most 128 MiB of HBM per device.

v0:
```python
import jax
import jax.numpy as jnp
from jax import lax
from jax.sharding import PartitionSpec as P

B = 128


def shards(lower_cols, pivot_rows, pattern, panel_in, diag_in):
    col_index = lax.axis_index("col")
    k_local = lower_cols.shape[0] // B
    targets = pattern.shape[0]
    own_targets = diag_in.shape[0]
    width = panel_in.shape[1]
    whole_pivot = lax.all_gather(pivot_rows, "row", axis=0, tiled=True)
    local_pattern = lax.dynamic_slice_in_dim(pattern, col_index * k_local, k_local, 1).astype(
        jnp.float32
    )
    masked = whole_pivot.reshape(targets, B, k_local, B) * local_pattern[:, None, :, None]
    masked = masked.reshape(targets * B, k_local * B)
    update = lax.psum_scatter(
        jnp.dot(
            masked, lower_cols, precision=lax.Precision.HIGHEST, preferred_element_type=jnp.float32
        ),
        "col",
        scatter_dimension=0,
        tiled=True,
    )
    blocks = masked.reshape(targets, B, k_local * B)
    partial_diag = jnp.einsum("jak,jbk->jab", blocks, blocks, precision=lax.Precision.HIGHEST)
    dsum = lax.psum_scatter(partial_diag, "col", scatter_dimension=0, tiled=True)
    factor = jnp.linalg.cholesky(diag_in - dsum)
    residue = (panel_in - update).reshape(own_targets, B, width)
    solved = lax.linalg.triangular_solve(factor, residue, left_side=True, lower=True)
    return (solved.reshape(own_targets * B, width), factor)


def solution(mesh):
    in_specs = (P("col", "row"), P("row", "col"), P(), P("col", "row"), P("col", None, None))
    out_specs = (P("col", "row"), P("col", None, None))
    return jax.shard_map(shards, mesh=mesh, in_specs=in_specs, out_specs=out_specs, check_vma=False)
```

profile of v0, /device:TPU:2, one launch (start us, length us, event | category | flops | bytes accessed | tf_op | source)
XLA Modules:
  0.0 266.4 jit_solution(10246708308004626296)
XLA Ops:
  7.2 0.0 copy-start
  7.2 0.0 all-gather.2.cloned.1.call-start
  7.2 0.7 all-gather.2.cloned.1.call-update
  7.9 0.0 reduce-scatter.3.cloned.1.call-start
  8.0 0.7 dynamic-slice_convert_fusion
  8.7 0.1 copy.13
  8.8 0.1 mul.24
  8.9 80.3 %all-gather.2.cloned.1.call-done = f32[8192,256]{1,0:T(8,128)} async-done(((f32[512,256]{1,0:T(8,128)}), f32[8192,256]{1,0:T(8,128)}) %all-gather.2.cloned.1.call-update) | async-done | bytes 8388624 | tf_op jit(solution)/shard_map/all_gather | solution.py:15
  89.2 16.6 %fusion.2 = f32[64,128,128]{1,2,0:T(8,128)} fusion(f32[64,128,256]{2,1,0:T(8,128)} %bitcast.23, f32[64,256]{1,0:T(8,128)S(1)} %bitcast.26), kind=kOutput, calls=%fused_computation.3 | convolution fusion | flops 3223322624 | bytes 12648448 | tf_op jit(solution)/shard_map/jak,jbk->jab/dot_general | solution.py:30
  105.8 0.0 reduce-scatter.3.cloned.1.call-update
  105.9 0.0 reduce-scatter.5.cloned.1.call-start
  105.9 5.4 %mul.28 = f32[64,128,2,128]{3,2,1,0:T(2,128)} broadcast(f32[64,2]{1,0:T(8,128)S(1)} %copy.13), dimensions={0,2} | broadcast | bytes 8389120 | tf_op jit(solution)/shard_map/mul | solution.py:19
  111.3 0.0 copy-done
  111.3 0.0 copy-start.2
  111.3 0.0 copy-start.1
  111.3 12.2 %fusion = f32[8192,128]{1,0:T(8,128)} fusion(f32[256,128]{1,0:T(8,128)S(1)} %copy-done, f32[8192,256]{1,0:T(8,128)} %all-gather.2.cloned.1.call-done, f32[1024,8,2,128]{3,2,1,0:T(2,128)} %bitcast.24), kind=kOutput, calls=%fused_computation.1 | convolution fusion | flops 3223322624 | bytes 21102592 | tf_op jit(solution)/shard_map/dot_general | solution.py:22
  123.5 0.0 reduce-scatter.5.cloned.1.call-update
  123.6 0.0 copy-done.2
  123.6 0.1 copy.15
  123.8 45.4 %reduce-scatter.3.cloned.1.call-done = f32[4,128,128]{1,2,0:T(8,128)} async-done(((f32[64,128,128]{1,2,0:T(8,128)}), f32[4,128,128]{1,2,0:T(8,128)}) %reduce-scatter.3.cloned.1.call-update) | async-done | bytes 262160 | tf_op jit(solution)/shard_map/reduce_scatter | solution.py:31
  169.2 1.0 sub.6
  170.2 0.1 copy.16
  170.3 46.9 %custom-call.7 = f32[4,128,128]{2,1,0:T(8,128)S(1)} custom-call(f32[4,128,128]{2,1,0:T(8,128)S(1)} %fusion.7), custom_call_target="Cholesky" | custom-call | tf_op jit(solution)/shard_map/jit(cholesky)/cholesky | solution.py:32
  217.3 0.1 compare_reduce_fusion
  217.4 0.8 select_bitcast_fusion
  218.2 39.3 %custom-call.8 = f32[4,1,128,128]{2,3,1,0:T(8,128)S(1)} custom-call(f32[4,1,128,128]{3,2,1,0:T(8,128)S(1)} %get-tuple-element.2), custom_call_target="InvertDiagBlocksLowerTriangular" | custom-call | tf_op jit(solution)/shard_map/triangular_solve | solution.py:34
  257.5 0.0 reduce-scatter.5.cloned.1.call-done
  257.5 0.0 copy-done.1
  257.6 1.0 sub.7
  258.5 1.3 fusion.5
  (5 shorter events, 0.1 us)
Async XLA Ops:
  7.2 104.2 %copy-start = (f32[256,128]{1,0:T(8,128)S(1)}, f32[256,128]{1,0:T(8,128)}, u32[]{:S(2)}) copy-start(f32[256,128]{1,0:T(8,128)} %param.5) | copy-start | bytes 393220
  7.2 82.0 %all-gather.2.cloned.1.call-start = ((), (), s32[]{:S(2)}) async-start(), calls=%async_computation.2 | async-start | bytes 8912896 | tf_op jit(solution)/shard_map/all_gather | solution.py:15
  7.9 161.3 %reduce-scatter.3.cloned.1.call-start = ((), (), s32[]{:S(2)}) async-start(), calls=%async_computation.3 | async-start | bytes 4456448 | tf_op jit(solution)/shard_map/reduce_scatter | solution.py:31
  105.9 151.7 %reduce-scatter.5.cloned.1.call-start = ((), (), s32[]{:S(2)}) async-start(), calls=%async_computation.4 | async-start | bytes 4456448 | tf_op jit(solution)/shard_map/reduce_scatter | solution.py:21
  111.3 12.2 %copy-start.2 = (f32[4,128,128]{2,1,0:T(8,128)S(1)}, f32[4,128,128]{2,1,0:T(8,128)}, u32[]{:S(2)}) copy-start(f32[4,128,128]{2,1,0:T(8,128)} %param.9) | copy-start | bytes 786436
  111.3 146.2 %copy-start.1 = (f32[512,128]{1,0:T(8,128)S(1)}, f32[512,128]{1,0:T(8,128)}, u32[]{:S(2)}) copy-start(f32[512,128]{1,0:T(8,128)} %param.8) | copy-start | bytes 786436
Sparse Core Ops, SparseCore 0:
  10.4 78.7 all-gather.1
  106.0 63.1 reduce-scatter.2
  171.7 62.2 reduce-scatter.4
where the time goes:
time: 267 us; the launch traced here: 266 us
  waiting for transfers between devices  126 us (47%)
  other arithmetic  89.9 us (34%)
  matrix products  30.1 us (11%)
  between operations  13.9 us (5%)
  local copies, waits for them, and re-layouts  5.94 us (2%)
    all_gather x1, waiting for transfers between devices, shards(): whole_pivot = lax.all_gather(pivot_rows, 'row', axis=0, tiled=True)  80.3 us
    another operation x4, other arithmetic, shards(): factor = jnp.linalg.cholesky(diag_in - dsum)  47.1 us
    reduce_scatter x1, waiting for transfers between devices, shards(): lax.psum_scatter(partial_diag, 'col', scatter_dimension=0, tiled=True)  45.4 us
    another operation x3, other arithmetic, shards(): lax.linalg.triangular_solve(factor, residue, left_side=True, lower=True)  40.1 us
    dot_general x1, matrix products, shards(): jnp.einsum('jak,jbk->jab', blocks, blocks, precision=lax.Precision.HIGHEST)  16.6 us
    dot_general x1, matrix products, shards(): jnp.dot(masked, lower_cols, precision=lax.Precision.HIGHEST, preferred_el...  12.2 us
    mul x2, local copies, waits for them, and re-layouts, shards(): whole_pivot.reshape(targets, B, k_local, B)  5.56 us
  transfers between devices with their start and end apart: 3, of which 2 were waited for; matrix products, arithmetic and copies ran while one was open for 40% of the time, Pallas kernels for 0%

commit v1 on v0

--- a/solution.py
+++ b/solution.py
@@ -6,13 +6,34 @@
 B = 128
 
 
+def gather_around(x, axis, dim):
+    peers, index, span = (lax.axis_size(axis), lax.axis_index(axis), x.shape[dim])
+    ahead = [(i, (i + 1) % peers) for i in range(peers)]
+    behind = [(i, (i - 1) % peers) for i in range(peers)]
+    out = jnp.zeros((*x.shape[:dim], peers * span, *x.shape[dim + 1 :]), x.dtype)
+    out = lax.dynamic_update_slice_in_dim(out, x, index * span, axis=dim)
+    from_left = from_right = x
+    half = peers // 2
+    for step in range(1, half + 1):
+        from_left = lax.ppermute(from_left, axis, ahead)
+        out = lax.dynamic_update_slice_in_dim(
+            out, from_left, (index - step) % peers * span, axis=dim
+        )
+        if step < peers - half:
+            from_right = lax.ppermute(from_right, axis, behind)
+            out = lax.dynamic_update_slice_in_dim(
+                out, from_right, (index + step) % peers * span, axis=dim
+            )
+    return out
+
+
 def shards(lower_cols, pivot_rows, pattern, panel_in, diag_in):
     col_index = lax.axis_index("col")
     k_local = lower_cols.shape[0] // B
     targets = pattern.shape[0]
     own_targets = diag_in.shape[0]
     width = panel_in.shape[1]
-    whole_pivot = lax.all_gather(pivot_rows, "row", axis=0, tiled=True)
+    whole_pivot = gather_around(pivot_rows, "row", 0)
     local_pattern = lax.dynamic_slice_in_dim(pattern, col_index * k_local, k_local, 1).astype(
         jnp.float32
     )

time: 267 us -> 300 us (1.12)
  starting transfers between devices: 0.12 us -> 29.1 us
  local copies, waits for them, and re-layouts: 5.94 us -> 28.4 us
  waiting for transfers between devices: 126 us -> 108 us
    all_gather x1 -> x0, waiting for transfers between devices: 80.3 us -> none  [shards(): whole_pivot = lax.all_gather(pivot_rows, 'row', axis=0, tiled=True)]
    ppermute x0 -> x15, waiting for transfers between devices: none -> 55.8 us  [the longest x8 55.7 us: gather_around(): from_left = lax.ppermute(from_left, axis, ahead)]
    ppermute x0 -> x15, starting transfers between devices: none -> 29 us  [the longest x7 27.3 us: gather_around(): from_right = lax.ppermute(from_right, axis, behind)]
    dynamic_update_slice x0 -> x16, local copies, waits for them, and re-layouts: none -> 18.7 us  [the longest x8 9.91 us: gather_around(): lax.dynamic_update_slice_in_dim(out, from_left, (index - step) % peers *...]
    reduce_scatter x1, waiting for transfers between devices: 45.4 us -> 51.9 us  [shards(): lax.psum_scatter(partial_diag, 'col', scatter_dimension=0, tiled=True)]
    broadcast_in_dim x0 -> x1, local copies, waits for them, and re-layouts: none -> 3.78 us  [gather_around(): out = jnp.zeros((*x.shape[:dim], peers * span, *x.shape[dim + 1:]), x.dtype)]
  transfers between devices with their start and end apart: 3 -> 17, of which waited for: 2 -> 9; matrix products, arithmetic and copies ran while one was open for 40% -> 43% of each run, Pallas kernels for 0% -> 0%
where the time goes in v1:
time: 300 us
  waiting for transfers between devices  108 us (36%)
  other arithmetic  89.9 us (30%)
  matrix products  30.2 us (10%)
  starting transfers between devices  29.1 us (10%)
  local copies, waits for them, and re-layouts  28.4 us (9%)
  between operations  14.3 us (5%)
    ppermute x8, waiting for transfers between devices, gather_around(): from_left = lax.ppermute(from_left, axis, ahead)  55.7 us
    reduce_scatter x1, waiting for transfers between devices, shards(): lax.psum_scatter(partial_diag, 'col', scatter_dimension=0, tiled=True)  51.9 us
    another operation x4, other arithmetic, shards(): factor = jnp.linalg.cholesky(diag_in - dsum)  47.1 us
    another operation x3, other arithmetic, shards(): lax.linalg.triangular_solve(factor, residue, left_side=True, lower=True)  40.1 us
    ppermute x7, starting transfers between devices, gather_around(): from_right = lax.ppermute(from_right, axis, behind)  27.3 us
    dot_general x1, matrix products, shards(): jnp.einsum('jak,jbk->jab', blocks, blocks, precision=lax.Precision.HIGHEST)  16.6 us
    dot_general x1, matrix products, shards(): jnp.dot(masked, lower_cols, precision=lax.Precision.HIGHEST, preferred_el...  12.2 us
    dynamic_update_slice x8, local copies, waits for them, and re-layouts, gather_around(): lax.dynamic_update_slice_in_dim(out, from_left, (index - step) % peers *...  9.91 us
  transfers between devices with their start and end apart: 17, of which 9 were waited for; matrix products, arithmetic and copies ran while one was open for 43% of the time, Pallas kernels for 0%

profile of v1, /device:TPU:2, one launch (start us, length us, event | category | flops | bytes accessed | tf_op | source)
XLA Modules:
  0.0 299.5 jit_solution(12884865325463041097)
XLA Ops:
  7.2 1.7 collective-permute-start
  8.9 2.6 collective-permute-start.1
  11.4 11.8 %collective-permute-done = f32[512,256]{1,0:T(8,128)S(1)} collective-permute-done((f32[512,256]{1,0:T(8,128)}, f32[512,256]{1,0:T(8,128)S(1)}, u32[]{:S(2)}, u32[]{:S(2)}) %collective-permute-start) | collective-permute-done | bytes 524320 | tf_op jit(solution)/shard_map/ppermute | solution.py:18
  23.3 4.1 %collective-permute-start.3 = (f32[512,256]{1,0:T(8,128)S(1)}, f32[512,256]{1,0:T(8,128)S(1)}, u32[]{:S(2)}, u32[]{:S(2)}) collective-permute-start(f32[512,256]{1,0:T(8,128)S(1)} %collective-permute-done.1), channel_id=1, source_target_pairs={{0,15},{1,0},{2,1},{3,2},{4,3},{5,4},{6,5},{7,6},{8,7},{9,8},{10,9... | collective-permute-start | bytes 1572872 | tf_op jit(solution)/shard_map/ppermute | solution.py:23
  27.4 10.8 %collective-permute-done.2 = f32[512,256]{1,0:T(8,128)S(1)} collective-permute-done((f32[512,256]{1,0:T(8,128)S(1)}, f32[512,256]{1,0:T(8,128)S(1)}, u32[]{:S(2)}, u32[]{:S(2)}) %collective-permute-start.2) | collective-permute-done | bytes 524320 | tf_op jit(solution)/shard_map/ppermute | solution.py:18
  38.2 4.1 %collective-permute-start.5 = (f32[512,256]{1,0:T(8,128)S(1)}, f32[512,256]{1,0:T(8,128)S(1)}, u32[]{:S(2)}, u32[]{:S(2)}) collective-permute-start(f32[512,256]{1,0:T(8,128)S(1)} %collective-permute-done.3), channel_id=1, source_target_pairs={{0,15},{1,0},{2,1},{3,2},{4,3},{5,4},{6,5},{7,6},{8,7},{9,8},{10,9... | collective-permute-start | bytes 1572872 | tf_op jit(solution)/shard_map/ppermute | solution.py:23
  42.4 9.9 %collective-permute-done.4 = f32[512,256]{1,0:T(8,128)S(1)} collective-permute-done((f32[512,256]{1,0:T(8,128)S(1)}, f32[512,256]{1,0:T(8,128)S(1)}, u32[]{:S(2)}, u32[]{:S(2)}) %collective-permute-start.4) | collective-permute-done | bytes 524320 | tf_op jit(solution)/shard_map/ppermute | solution.py:18
  52.3 4.1 %collective-permute-start.7 = (f32[512,256]{1,0:T(8,128)S(1)}, f32[512,256]{1,0:T(8,128)}, u32[]{:S(2)}, u32[]{:S(2)}) collective-permute-start(f32[512,256]{1,0:T(8,128)S(1)} %collective-permute-done.5), channel_id=1, source_target_pairs={{0,15},{1,0},{2,1},{3,2},{4,3},{5,4},{6,5},{7,6},{8,7},{9,8},{10,9... | collective-permute-start | bytes 1572872 | tf_op jit(solution)/shard_map/ppermute | solution.py:23
  56.4 9.2 %collective-permute-done.6 = f32[512,256]{1,0:T(8,128)} collective-permute-done((f32[512,256]{1,0:T(8,128)S(1)}, f32[512,256]{1,0:T(8,128)}, u32[]{:S(2)}, u32[]{:S(2)}) %collective-permute-start.6) | collective-permute-done | bytes 524320 | tf_op jit(solution)/shard_map/ppermute | solution.py:18
  65.6 4.1 %collective-permute-start.9 = (f32[512,256]{1,0:T(8,128)}, f32[512,256]{1,0:T(8,128)}, u32[]{:S(2)}, u32[]{:S(2)}) collective-permute-start(f32[512,256]{1,0:T(8,128)} %collective-permute-done.7), channel_id=1, source_target_pairs={{0,15},{1,0},{2,1},{3,2},{4,3},{5,4},{6,5},{7,6},{8,7},{9,8},{10,9... | collective-permute-start | bytes 1572872 | tf_op jit(solution)/shard_map/ppermute | solution.py:23
  69.7 3.8 %broadcast_in_dim.8 = f32[8192,256]{1,0:T(8,128)} broadcast(f32[]{:T(128)} %constant.131.clone.1), dimensions={} | broadcast | bytes 8388612 | tf_op jit(solution)/shard_map/broadcast_in_dim | solution.py:13
  74.3 3.9 %collective-permute-done.8 = f32[512,256]{1,0:T(8,128)} collective-permute-done((f32[512,256]{1,0:T(8,128)}, f32[512,256]{1,0:T(8,128)}, u32[]{:S(2)}, u32[]{:S(2)}) %collective-permute-start.8) | collective-permute-done | bytes 524320 | tf_op jit(solution)/shard_map/ppermute | solution.py:18
  81.0 1.9 constant_dynamic-update-slice_fusion.12
  82.8 4.1 %collective-permute-start.11 = (f32[512,256]{1,0:T(8,128)}, f32[512,256]{1,0:T(8,128)S(1)}, u32[]{:S(2)}, u32[]{:S(2)}) collective-permute-start(f32[512,256]{1,0:T(8,128)} %collective-permute-done.9), channel_id=1, source_target_pairs={{0,15},{1,0},{2,1},{3,2},{4,3},{5,4},{6,5},{7,6},{8,7},{9,8},{10,9... | collective-permute-start | bytes 1572872 | tf_op jit(solution)/shard_map/ppermute | solution.py:23
  87.8 2.7 collective-permute-done.10
  92.2 1.9 constant_dynamic-update-slice_fusion.8
  94.1 1.9 constant_dynamic-update-slice_fusion.7
  96.1 4.1 %collective-permute-start.13 = (f32[512,256]{1,0:T(8,128)S(1)}, f32[512,256]{1,0:T(8,128)S(1)}, u32[]{:S(2)}, u32[]{:S(2)}) collective-permute-start(f32[512,256]{1,0:T(8,128)S(1)} %collective-permute-done.11), channel_id=1, source_target_pairs={{0,15},{1,0},{2,1},{3,2},{4,3},{5,4},{6,5},{7,6},{8,7},{9,8},{10,9... | collective-permute-start | bytes 1572872 | tf_op jit(solution)/shard_map/ppermute | solution.py:23
  100.2 1.9 constant_dynamic-update-slice_fusion.6
  102.1 1.3 collective-permute-done.12
  103.4 1.9 constant_dynamic-update-slice_fusion.5
  105.3 0.9 constant_dynamic-update-slice_fusion.4
  108.7 6.0 %collective-permute-done.14 = f32[512,256]{1,0:T(8,128)S(1)} collective-permute-done((f32[512,256]{1,0:T(8,128)S(1)}, f32[512,256]{1,0:T(8,128)S(1)}, u32[]{:S(2)}, u32[]{:S(2)}) %collective-permute-start.14) | collective-permute-done | bytes 524320 | tf_op jit(solution)/shard_map/ppermute | solution.py:18
  115.5 16.6 %fusion.2 = f32[64,128,128]{1,2,0:T(8,128)} fusion(f32[64,128,256]{2,1,0:T(8,128)} %bitcast, f32[64,256]{1,0:T(8,128)S(1)} %bitcast.25), kind=kOutput, calls=%fused_computation.3 | convolution fusion | flops 3223322624 | bytes 12648448 | tf_op jit(solution)/shard_map/jak,jbk->jab/dot_general | solution.py:51
  132.2 5.4 %mul.92 = f32[64,128,2,128]{3,2,1,0:T(2,128)} broadcast(f32[64,2]{1,0:T(8,128)S(1)} %copy.13), dimensions={0,2} | broadcast | bytes 8389120 | tf_op jit(solution)/shard_map/mul | solution.py:40
  137.7 12.2 %fusion = f32[8192,128]{1,0:T(8,128)} fusion(f32[256,128]{1,0:T(8,128)S(1)} %copy-done, f32[8192,256]{1,0:T(8,128)} %constant_dynamic-update-slice_fusion, f32[1024,8,2,128]{3,2,1,0:T(2,128)} %bitcast.23), kind=kOutput, calls=%fused_computation.1 | convolution fusion | flops 3223322624 | bytes 21102592 | tf_op jit(solution)/shard_map/dot_general | solution.py:43
  150.1 51.9 %reduce-scatter.3.cloned.1.call-done = f32[4,128,128]{1,2,0:T(8,128)} async-done(((f32[64,128,128]{1,2,0:T(8,128)}), f32[4,128,128]{1,2,0:T(8,128)}) %reduce-scatter.3.cloned.1.call-update) | async-done | bytes 262160 | tf_op jit(solution)/shard_map/reduce_scatter | solution.py:52
  202.0 1.0 sub.38
  203.2 46.9 %custom-call.7 = f32[4,128,128]{2,1,0:T(8,128)S(1)} custom-call(f32[4,128,128]{2,1,0:T(8,128)S(1)} %fusion.7), custom_call_target="Cholesky" | custom-call | tf_op jit(solution)/shard_map/jit(cholesky)/cholesky | solution.py:53
  251.1 39.3 %custom-call.8 = f32[4,1,128,128]{2,3,1,0:T(8,128)S(1)} custom-call(f32[4,1,128,128]{3,2,1,0:T(8,128)S(1)} %get-tuple-element.2), custom_call_target="InvertDiagBlocksLowerTriangular" | custom-call | tf_op jit(solution)/shard_map/triangular_solve | solution.py:55
  290.4 1.0 sub.39
  291.4 1.3 fusion.5
  (51 shorter events, 10.8 us)
Async XLA Ops:
  7.2 130.5 %copy-start = (f32[256,128]{1,0:T(8,128)S(1)}, f32[256,128]{1,0:T(8,128)}, u32[]{:S(2)}) copy-start(f32[256,128]{1,0:T(8,128)} %param.5) | copy-start | bytes 393220
  7.2 66.3 %copy-start.1 = (f32[512,256]{1,0:T(8,128)S(1)}, f32[512,256]{1,0:T(8,128)}, u32[]{:S(2)}) copy-start(f32[512,256]{1,0:T(8,128)} %param.6) | copy-start | bytes 1572868
  7.2 194.8 %reduce-scatter.3.cloned.1.call-start = ((), (), s32[]{:S(2)}) async-start(), calls=%async_computation.2 | async-start | bytes 4456448 | tf_op jit(solution)/shard_map/reduce_scatter | solution.py:52
  7.2 16.1 %collective-permute-start = (f32[512,256]{1,0:T(8,128)}, f32[512,256]{1,0:T(8,128)S(1)}, u32[]{:S(2)}, u32[]{:S(2)}) collective-permute-start(f32[512,256]{1,0:T(8,128)} %param.6), channel_id=1, source_target_pairs={{0,1},{1,2},{2,3},{3,4},{4,5},{5,6},{6,7},{7,8},{8,9},{9,10},{10,1... | collective-permute-start | bytes 1572872 | tf_op jit(solution)/shard_map/ppermute | solution.py:18
  8.9 14.4 %collective-permute-start.1 = (f32[512,256]{1,0:T(8,128)}, f32[512,256]{1,0:T(8,128)S(1)}, u32[]{:S(2)}, u32[]{:S(2)}) collective-permute-start(f32[512,256]{1,0:T(8,128)} %param.6), channel_id=1, source_target_pairs={{0,15},{1,0},{2,1},{3,2},{4,3},{5,4},{6,5},{7,6},{8,7},{9,8},{10,9... | collective-permute-start | bytes 1572872 | tf_op jit(solution)/shard_map/ppermute | solution.py:23
  23.3 14.9 %collective-permute-start.2 = (f32[512,256]{1,0:T(8,128)S(1)}, f32[512,256]{1,0:T(8,128)S(1)}, u32[]{:S(2)}, u32[]{:S(2)}) collective-permute-start(f32[512,256]{1,0:T(8,128)S(1)} %collective-permute-done), channel_id=1, source_target_pairs={{0,1},{1,2},{2,3},{3,4},{4,5},{5,6},{6,7},{7,8},{8,9},{9,10},{10,1... | collective-permute-start | bytes 1572872 | tf_op jit(solution)/shard_map/ppermute | solution.py:18
  23.3 14.9 %collective-permute-start.3 = (f32[512,256]{1,0:T(8,128)S(1)}, f32[512,256]{1,0:T(8,128)S(1)}, u32[]{:S(2)}, u32[]{:S(2)}) collective-permute-start(f32[512,256]{1,0:T(8,128)S(1)} %collective-permute-done.1), channel_id=1, source_target_pairs={{0,15},{1,0},{2,1},{3,2},{4,3},{5,4},{6,5},{7,6},{8,7},{9,8},{10,9... | collective-permute-start | bytes 1572872 | tf_op jit(solution)/shard_map/ppermute | solution.py:23
  38.2 27.4 %copy-start.2 = (f32[512,256]{1,0:T(8,128)}, f32[512,256]{1,0:T(8,128)S(1)}, u32[]{:S(2)}) copy-start(f32[512,256]{1,0:T(8,128)S(1)} %collective-permute-done.2) | copy-start | bytes 1572868
  38.2 14.1 %collective-permute-start.4 = (f32[512,256]{1,0:T(8,128)S(1)}, f32[512,256]{1,0:T(8,128)S(1)}, u32[]{:S(2)}, u32[]{:S(2)}) collective-permute-start(f32[512,256]{1,0:T(8,128)S(1)} %collective-permute-done.2), channel_id=1, source_target_pairs={{0,1},{1,2},{2,3},{3,4},{4,5},{5,6},{6,7},{7,8},{8,9},{9,10},{10,1... | collective-permute-start | bytes 1572872 | tf_op jit(solution)/shard_map/ppermute | solution.py:18
  38.2 14.1 %collective-permute-start.5 = (f32[512,256]{1,0:T(8,128)S(1)}, f32[512,256]{1,0:T(8,128)S(1)}, u32[]{:S(2)}, u32[]{:S(2)}) collective-permute-start(f32[512,256]{1,0:T(8,128)S(1)} %collective-permute-done.3), channel_id=1, source_target_pairs={{0,15},{1,0},{2,1},{3,2},{4,3},{5,4},{6,5},{7,6},{8,7},{9,8},{10,9... | collective-permute-start | bytes 1572872 | tf_op jit(solution)/shard_map/ppermute | solution.py:23
  52.3 13.3 %collective-permute-start.6 = (f32[512,256]{1,0:T(8,128)S(1)}, f32[512,256]{1,0:T(8,128)}, u32[]{:S(2)}, u32[]{:S(2)}) collective-permute-start(f32[512,256]{1,0:T(8,128)S(1)} %collective-permute-done.4), channel_id=1, source_target_pairs={{0,1},{1,2},{2,3},{3,4},{4,5},{5,6},{6,7},{7,8},{8,9},{9,10},{10,1... | collective-permute-start | bytes 1572872 | tf_op jit(solution)/shard_map/ppermute | solution.py:18
  52.3 13.3 %collective-permute-start.7 = (f32[512,256]{1,0:T(8,128)S(1)}, f32[512,256]{1,0:T(8,128)}, u32[]{:S(2)}, u32[]{:S(2)}) collective-permute-start(f32[512,256]{1,0:T(8,128)S(1)} %collective-permute-done.5), channel_id=1, source_target_pairs={{0,15},{1,0},{2,1},{3,2},{4,3},{5,4},{6,5},{7,6},{8,7},{9,8},{10,9... | collective-permute-start | bytes 1572872 | tf_op jit(solution)/shard_map/ppermute | solution.py:23
  65.6 12.7 %collective-permute-start.8 = (f32[512,256]{1,0:T(8,128)}, f32[512,256]{1,0:T(8,128)}, u32[]{:S(2)}, u32[]{:S(2)}) collective-permute-start(f32[512,256]{1,0:T(8,128)} %collective-permute-done.6), channel_id=1, source_target_pairs={{0,1},{1,2},{2,3},{3,4},{4,5},{5,6},{6,7},{7,8},{8,9},{9,10},{10,1... | collective-permute-start | bytes 1572872 | tf_op jit(solution)/shard_map/ppermute | solution.py:18
  65.6 17.2 %collective-permute-start.9 = (f32[512,256]{1,0:T(8,128)}, f32[512,256]{1,0:T(8,128)}, u32[]{:S(2)}, u32[]{:S(2)}) collective-permute-start(f32[512,256]{1,0:T(8,128)} %collective-permute-done.7), channel_id=1, source_target_pairs={{0,15},{1,0},{2,1},{3,2},{4,3},{5,4},{6,5},{7,6},{8,7},{9,8},{10,9... | collective-permute-start | bytes 1572872 | tf_op jit(solution)/shard_map/ppermute | solution.py:23
  78.3 12.3 %collective-permute-start.10 = (f32[512,256]{1,0:T(8,128)}, f32[512,256]{1,0:T(8,128)S(1)}, u32[]{:S(2)}, u32[]{:S(2)}) collective-permute-start(f32[512,256]{1,0:T(8,128)} %collective-permute-done.8), channel_id=1, source_target_pairs={{0,1},{1,2},{2,3},{3,4},{4,5},{5,6},{6,7},{7,8},{8,9},{9,10},{10,1... | collective-permute-start | bytes 1572872 | tf_op jit(solution)/shard_map/ppermute | solution.py:18
  82.8 13.2 %collective-permute-start.11 = (f32[512,256]{1,0:T(8,128)}, f32[512,256]{1,0:T(8,128)S(1)}, u32[]{:S(2)}, u32[]{:S(2)}) collective-permute-start(f32[512,256]{1,0:T(8,128)} %collective-permute-done.9), channel_id=1, source_target_pairs={{0,15},{1,0},{2,1},{3,2},{4,3},{5,4},{6,5},{7,6},{8,7},{9,8},{10,9... | collective-permute-start | bytes 1572872 | tf_op jit(solution)/shard_map/ppermute | solution.py:23
  90.6 12.8 %collective-permute-start.12 = (f32[512,256]{1,0:T(8,128)S(1)}, f32[512,256]{1,0:T(8,128)S(1)}, u32[]{:S(2)}, u32[]{:S(2)}) collective-permute-start(f32[512,256]{1,0:T(8,128)S(1)} %collective-permute-done.10), channel_id=1, source_target_pairs={{0,1},{1,2},{2,3},{3,4},{4,5},{5,6},{6,7},{7,8},{8,9},{9,10},{10,1... | collective-permute-start | bytes 1572872 | tf_op jit(solution)/shard_map/ppermute | solution.py:18
  96.1 11.8 %collective-permute-start.13 = (f32[512,256]{1,0:T(8,128)S(1)}, f32[512,256]{1,0:T(8,128)S(1)}, u32[]{:S(2)}, u32[]{:S(2)}) collective-permute-start(f32[512,256]{1,0:T(8,128)S(1)} %collective-permute-done.11), channel_id=1, source_target_pairs={{0,15},{1,0},{2,1},{3,2},{4,3},{5,4},{6,5},{7,6},{8,7},{9,8},{10,9... | collective-permute-start | bytes 1572872 | tf_op jit(solution)/shard_map/ppermute | solution.py:23
  103.4 11.3 %collective-permute-start.14 = (f32[512,256]{1,0:T(8,128)S(1)}, f32[512,256]{1,0:T(8,128)S(1)}, u32[]{:S(2)}, u32[]{:S(2)}) collective-permute-start(f32[512,256]{1,0:T(8,128)S(1)} %collective-permute-done.12), channel_id=1, source_target_pairs={{0,1},{1,2},{2,3},{3,4},{4,5},{5,6},{6,7},{7,8},{8,9},{9,10},{10,1... | collective-permute-start | bytes 1572872 | tf_op jit(solution)/shard_map/ppermute | solution.py:18
  132.2 158.2 %reduce-scatter.5.cloned.1.call-start = ((), (), s32[]{:S(2)}) async-start(), calls=%async_computation.3 | async-start | bytes 4456448 | tf_op jit(solution)/shard_map/reduce_scatter | solution.py:42
  137.7 12.3 %copy-start.4 = (f32[4,128,128]{2,1,0:T(8,128)S(1)}, f32[4,128,128]{2,1,0:T(8,128)}, u32[]{:S(2)}) copy-start(f32[4,128,128]{2,1,0:T(8,128)} %param.9) | copy-start | bytes 786436
  137.7 152.7 %copy-start.3 = (f32[512,128]{1,0:T(8,128)S(1)}, f32[512,128]{1,0:T(8,128)}, u32[]{:S(2)}) copy-start(f32[512,128]{1,0:T(8,128)} %param.8) | copy-start | bytes 786436
Sparse Core Ops, SparseCore 0:
  132.3 69.6 reduce-scatter.2
  204.6 62.5 reduce-scatter.4
